TPU v7x, 128 devices: a whole 4x4x4 slice. The times are simulated.
128 devices in a mesh: dp: 4 (over x_lo, core), code: 32 (over z, y, x_hi).
Axes of the slice: x: 4 (x_hi: 2, x_lo: 2; x = x_hi * 2 + x_lo), y: 4, z: 4, core: 2. Of those that a mesh axis runs over, the one named last changes fastest.
Arguments:
- image_tokens: bfloat16 [16384, 1024], P(('dp', 'code')), may hold values from -6 to 6
- w_in: bfloat16 [1024, 4096], replicated, as said below
- w_out: bfloat16 [4096, 1024], replicated, as said below
- w_proj: bfloat16 [1024, 256], replicated, as said below
- codebook: bfloat16 [131072, 256], P('code'), may hold values from -6 to 6
- inv_temp: float32 [16384], replicated, may hold values from 4 to 240, as said below
- prior_mass: float32 [131072], P('code'), may hold values from 0.02 to 0.2
Outputs:
- refit_codes: float32 [131072, 256], P(('code', 'dp'))
- code_mass: float32 [131072], P(('code', 'dp'))
Inputs may be any that keep to these rules, and one draw needn't show every extreme that they name: `inv_temp`: positive inverse temperatures. `w_in`: every entry lies within 6 / sqrt(1024) of zero. `w_out`: every entry lies within 6 / sqrt(4096) of zero. `w_proj`: every entry lies within 6 / sqrt(1024) of zero.
All inputs are finite; a program needn't handle non-finite values.
Results may differ from a plain program's by a relative error of at most 0.003.
The roundings to bfloat16 on the way count: a program that leaves them out, or rounds other values in their place, can miss the bound.
Values may be sent and summed in bfloat16 or wider, within the bound.
A program may use at most 128 MiB of HBM per device.

v0:
```python
import math
import jax
import jax.numpy as jnp
from jax import lax
from jax.sharding import PartitionSpec as P


def encode(image_tokens, w_in, w_out, w_proj):
    tokens_f = image_tokens.astype(jnp.float32)
    mean = jnp.mean(tokens_f, axis=1, keepdims=True)
    centered = tokens_f - mean
    var = jnp.mean(centered * centered, axis=1, keepdims=True)
    normed = (centered * lax.rsqrt(var + 1e-06)).astype(jnp.bfloat16)
    hidden = jax.nn.gelu(
        jnp.dot(normed, w_in, preferred_element_type=jnp.float32), approximate=False
    ).astype(jnp.bfloat16)
    encoded = (tokens_f + jnp.dot(hidden, w_out, preferred_element_type=jnp.float32)).astype(
        jnp.bfloat16
    )
    projected = jnp.dot(encoded, w_proj, preferred_element_type=jnp.float32)
    width = projected.shape[1]
    factor = jnp.sqrt(width / (jnp.sum(projected * projected, axis=1, keepdims=True) + 1e-06))
    return (projected * factor).astype(jnp.bfloat16)


def in_blocks(func, arrays):
    rows = arrays[0].shape[0]
    block = math.gcd(rows, 512)
    shaped = tuple((item.reshape((rows // block, block) + item.shape[1:]) for item in arrays))
    results = lax.map(lambda items: func(*items), shaped)
    return jax.tree.map(lambda item: item.reshape((rows,) + item.shape[2:]), results)


def weighted_sums(token_rows, scale_rows, norm_rows, code_rows):
    rows = token_rows.shape[0]
    width = token_rows.shape[1]
    block = math.gcd(rows, 512)
    count = rows // block

    def accumulate(carry, items):
        token_block, scale_block, norm_block = items
        logits = (
            jnp.dot(token_block, code_rows.T, preferred_element_type=jnp.float32)
            * scale_block[:, None]
        )
        resp = jnp.exp(logits - norm_block[:, None]).astype(jnp.bfloat16)
        sums = carry[0] + lax.dot_general(
            resp, token_block, (((0,), (0,)), ((), ())), preferred_element_type=jnp.float32
        )
        mass = carry[1] + jnp.sum(resp.astype(jnp.float32), axis=0)
        return ((sums, mass), None)

    start = (
        jnp.zeros((code_rows.shape[0], width), jnp.float32),
        jnp.zeros((code_rows.shape[0],), jnp.float32),
    )
    items = (
        token_rows.reshape(count, block, width),
        scale_rows.reshape(count, block),
        norm_rows.reshape(count, block),
    )
    (sums, mass), _ = lax.scan(accumulate, start, items)
    return (sums, mass)


def local(image_tokens, w_in, w_out, w_proj, codebook, inv_temp, prior_mass):
    unit_tokens = encode(image_tokens, w_in, w_out, w_proj)
    width = unit_tokens.shape[1]
    codebook_f = codebook.astype(jnp.float32)
    unit_codes = (
        codebook_f * lax.rsqrt(jnp.mean(codebook_f * codebook_f, axis=1, keepdims=True) + 1e-06)
    ).astype(jnp.bfloat16)
    group_rows = unit_tokens.shape[0] * lax.axis_size("code")
    group_index = lax.axis_index("dp")
    all_scale = inv_temp * (1.0 / width)
    group_scale = lax.dynamic_slice_in_dim(all_scale, group_index * group_rows, group_rows)

    def block_stats(token_block, scale_block):
        logits = (
            jnp.dot(token_block, unit_codes.T, preferred_element_type=jnp.float32)
            * scale_block[:, None]
        )
        peak = jnp.max(logits, axis=1)
        return (peak, jnp.sum(jnp.exp(logits - peak[:, None]), axis=1))

    piece = lax.all_gather(unit_tokens, "code", axis=0, tiled=True)
    peak, total = in_blocks(block_stats, (piece, group_scale))
    local_peak = peak
    local_total = total
    peak = lax.pmax(local_peak, "code")
    total = lax.psum(local_total * jnp.exp(local_peak - peak), "code")
    lognorm = peak + jnp.log(total)
    owned = codebook.shape[0] // lax.axis_size("dp")
    sums, mass = weighted_sums(piece, group_scale, lognorm, unit_codes)
    sums, mass = (
        lax.psum_scatter(sums, "dp", scatter_dimension=0, tiled=True),
        lax.psum_scatter(mass, "dp", scatter_dimension=0, tiled=True),
    )
    own_book = lax.dynamic_slice_in_dim(codebook_f, group_index * owned, owned)
    own_prior = lax.dynamic_slice_in_dim(prior_mass, group_index * owned, owned)
    refit = (own_prior[:, None] * own_book + sums) / (own_prior + mass)[:, None]
    return (refit, mass)


def solution(mesh):
    placed = (P(("dp", "code"), None), P(), P(), P(), P("code", None), P(), P("code"))
    return jax.shard_map(
        local,
        mesh=mesh,
        in_specs=placed,
        out_specs=(P(("code", "dp"), None), P(("code", "dp"))),
        check_vma=False,
    )
```

profile of v0, /device:TPU:1, one launch (start us, length us, event | category | flops | bytes accessed | tf_op | source)
XLA Modules:
  0.0 665.6 jit_solution(4588213453708250442)
XLA Ops:
  10.5 6.2 fusion.28
  22.9 1.6 erfc.277
  26.0 1.6 erfc.283
  27.6 1.6 erfc.286
  30.8 1.6 erfc.292
  35.4 1.6 mul.100
  38.5 18.3 %multiply_reduce_fusion.2 = (f32[128]{0:T(128)S(1)}, f32[128,256]{1,0:T(8,128)S(1)}) fusion(bf16[1024,256]{1,0:T(8,128)(2,1)S(1)} %copy-done, f32[128,1024]{1,0:T(8,128)S(1)} %convert_element_type.28, bf16[4096,1024]{1,0:T(8,128)(2,1)} %param.13, f32[128,4096]{1,0:T(8,128)} %erfc.292, f32[128,4096]{1,0:T(8,128)} %erfc.290, f32[128,4096]{1,0:T(8,128)} %erfc.301, ...), kind=kOutput, calls=%fused_computation.54 | convolution fusion | flops 1175256960 | bytes 41026048 | tf_op jit(solution)/shard_map/dot_general | solution.py:20
  60.9 68.3 %all-gather.2.cloned.1.call-done = bf16[4096,256]{1,0:T(8,128)(2,1)} async-done(((bf16[128,256]{1,0:T(8,128)(2,1)}), bf16[4096,256]{1,0:T(8,128)(2,1)}) %all-gather.2.cloned.1.call-update) | async-done | bytes 2097168 | tf_op jit(solution)/shard_map/all_gather | solution.py:86
  129.2 34.2 %while.25 = (s32[]{:T(128)}, f32[8,512]{1,0:T(8,128)S(1)}, f32[8,512]{1,0:T(8,128)S(1)}, bf16[8,512,256]{2,1,0:T(8,128)(2,1)}, bf16[4096,256]{1,0:T(8,128)(2,1)S...) while((s32[]{:T(128)}, f32[8,512]{1,0:T(8,128)S(1)}, f32[8,512]{1,0:T(8,128)S(1)}, ...), condition=%wide.region_7.8_spmd, body=%wide.region_4.7_spmd.sunk | while | flops 1084226560 | bytes 19159648 | solution.py:30
  129.2 2.3 multiply_reduce_fusion.4
  131.6 1.8 exponential_reduce_fusion.2
  133.5 2.3 multiply_reduce_fusion.4
  135.8 1.8 exponential_reduce_fusion.2
  137.8 2.3 multiply_reduce_fusion.4
  140.1 1.8 exponential_reduce_fusion.2
  142.1 2.3 multiply_reduce_fusion.4
  144.4 1.8 exponential_reduce_fusion.2
  146.3 2.3 multiply_reduce_fusion.4
  148.7 1.8 exponential_reduce_fusion.2
  150.6 2.3 multiply_reduce_fusion.4
  153.0 1.8 exponential_reduce_fusion.2
  154.9 2.3 multiply_reduce_fusion.4
  157.2 1.8 exponential_reduce_fusion.2
  159.2 2.3 multiply_reduce_fusion.4
  161.5 1.8 exponential_reduce_fusion.2
  163.5 153.2 %pmax.7 = f32[4096]{0:T(1024)S(1)} all-reduce(f32[4096]{0:T(1024)S(1)} %bitcast.56), channel_id=1, replica_groups=mesh['dp'=4,'code'=32] {'code'}, use_global_device_ids=true, to_apply=%region_8.9 | all-reduce | flops 4096 | bytes 32768 | tf_op jit(solution)/shard_map/pmax | solution.py:90
  316.7 149.6 %psum.7 = f32[4096]{0:T(1024)S(1)} all-reduce(f32[4096]{0:T(1024)S(1)} %exponential_multiply_fusion), channel_id=1, replica_groups=mesh['dp'=4,'code'=32] {'code'}, use_global_device_ids=true, to_apply=%region_9.10 | all-reduce | flops 4096 | bytes 32768 | tf_op jit(solution)/shard_map/psum | solution.py:91
  466.3 91.9 %while.26 = (s32[]{:T(128)}, f32[4096,256]{1,0:T(8,128)}, f32[4096]{0:T(1024)S(1)}, bf16[8,512,256]{2,1,0:T(8,128)(2,1)}, bf16[4096,256]{1,0:T(8,128)(2,1)S(1)},...) while((s32[]{:T(128)}, f32[4096,256]{1,0:T(8,128)}, ...), condition=%wide.region_12.13_spmd.clone, body=%wide.region_10.12_spmd.clone.sunk | while | flops 2160070656 | bytes 19477612 | solution.py:62
  466.3 4.9 convert_reduce_fusion.3
  471.2 5.4 convolution_add_fusion.3
  476.7 4.9 convert_reduce_fusion.3
  481.5 6.8 %convolution_add_fusion.3 = f32[4096,256]{1,0:T(8,128)} fusion(bf16[512,4096]{1,0:T(8,128)(2,1)} %get-tuple-element.228, f32[4096,256]{1,0:T(8,128)} %get-tuple-element.264, pred[]{:T(512)S(6)} %compare.3, bf16[8,512,256]{2,1,0:T(8,128)(2,1)} %get-tuple-element.275, s32[]{:T(128)} %get-tuple-element.263), kind=kOutput, calls=%fused_computation.9.clone.1 | convolution fusion | flops 1075838976 | bytes 12845569 | tf_op jit(solution)/shard_map/while/body/eval_jaxpr/dot_general | solution.py:47
  488.3 4.9 convert_reduce_fusion.3
  493.2 6.8 %convolution_add_fusion.3 = f32[4096,256]{1,0:T(8,128)} fusion(bf16[512,4096]{1,0:T(8,128)(2,1)} %get-tuple-element.228, f32[4096,256]{1,0:T(8,128)} %get-tuple-element.264, pred[]{:T(512)S(6)} %compare.3, bf16[8,512,256]{2,1,0:T(8,128)(2,1)} %get-tuple-element.275, s32[]{:T(128)} %get-tuple-element.263), kind=kOutput, calls=%fused_computation.9.clone.1 | convolution fusion | flops 1075838976 | bytes 12845569 | tf_op jit(solution)/shard_map/while/body/eval_jaxpr/dot_general | solution.py:47
  499.9 4.9 convert_reduce_fusion.3
  504.8 6.8 %convolution_add_fusion.3 = f32[4096,256]{1,0:T(8,128)} fusion(bf16[512,4096]{1,0:T(8,128)(2,1)} %get-tuple-element.228, f32[4096,256]{1,0:T(8,128)} %get-tuple-element.264, pred[]{:T(512)S(6)} %compare.3, bf16[8,512,256]{2,1,0:T(8,128)(2,1)} %get-tuple-element.275, s32[]{:T(128)} %get-tuple-element.263), kind=kOutput, calls=%fused_computation.9.clone.1 | convolution fusion | flops 1075838976 | bytes 12845569 | tf_op jit(solution)/shard_map/while/body/eval_jaxpr/dot_general | solution.py:47
  511.6 4.9 convert_reduce_fusion.3
  516.5 6.8 %convolution_add_fusion.3 = f32[4096,256]{1,0:T(8,128)} fusion(bf16[512,4096]{1,0:T(8,128)(2,1)} %get-tuple-element.228, f32[4096,256]{1,0:T(8,128)} %get-tuple-element.264, pred[]{:T(512)S(6)} %compare.3, bf16[8,512,256]{2,1,0:T(8,128)(2,1)} %get-tuple-element.275, s32[]{:T(128)} %get-tuple-element.263), kind=kOutput, calls=%fused_computation.9.clone.1 | convolution fusion | flops 1075838976 | bytes 12845569 | tf_op jit(solution)/shard_map/while/body/eval_jaxpr/dot_general | solution.py:47
  523.2 4.9 convert_reduce_fusion.3
  528.1 6.8 %convolution_add_fusion.3 = f32[4096,256]{1,0:T(8,128)} fusion(bf16[512,4096]{1,0:T(8,128)(2,1)} %get-tuple-element.228, f32[4096,256]{1,0:T(8,128)} %get-tuple-element.264, pred[]{:T(512)S(6)} %compare.3, bf16[8,512,256]{2,1,0:T(8,128)(2,1)} %get-tuple-element.275, s32[]{:T(128)} %get-tuple-element.263), kind=kOutput, calls=%fused_computation.9.clone.1 | convolution fusion | flops 1075838976 | bytes 12845569 | tf_op jit(solution)/shard_map/while/body/eval_jaxpr/dot_general | solution.py:47
  534.9 4.9 convert_reduce_fusion.3
  539.8 6.8 %convolution_add_fusion.3 = f32[4096,256]{1,0:T(8,128)} fusion(bf16[512,4096]{1,0:T(8,128)(2,1)} %get-tuple-element.228, f32[4096,256]{1,0:T(8,128)} %get-tuple-element.264, pred[]{:T(512)S(6)} %compare.3, bf16[8,512,256]{2,1,0:T(8,128)(2,1)} %get-tuple-element.275, s32[]{:T(128)} %get-tuple-element.263), kind=kOutput, calls=%fused_computation.9.clone.1 | convolution fusion | flops 1075838976 | bytes 12845569 | tf_op jit(solution)/shard_map/while/body/eval_jaxpr/dot_general | solution.py:47
  546.5 4.9 convert_reduce_fusion.3
  551.4 6.8 %convolution_add_fusion.3 = f32[4096,256]{1,0:T(8,128)} fusion(bf16[512,4096]{1,0:T(8,128)(2,1)} %get-tuple-element.228, f32[4096,256]{1,0:T(8,128)} %get-tuple-element.264, pred[]{:T(512)S(6)} %compare.3, bf16[8,512,256]{2,1,0:T(8,128)(2,1)} %get-tuple-element.275, s32[]{:T(128)} %get-tuple-element.263), kind=kOutput, calls=%fused_computation.9.clone.1 | convolution fusion | flops 1075838976 | bytes 12845569 | tf_op jit(solution)/shard_map/while/body/eval_jaxpr/dot_general | solution.py:47
  559.8 2.3 convert_element_type.27
  563.3 68.3 %all-reduce = f32[4096]{0:T(1024)S(1)} all-reduce(f32[4096]{0:T(1024)S(1)} %get-tuple-element.76), channel_id=3, replica_groups=mesh['dp'=4,'code'=32] {'dp'}, use_global_device_ids=true, to_apply=%region_14.15.clone | all-reduce | flops 4096 | bytes 32768
  632.8 23.1 %reduce-scatter.2.cloned.1.call-done = f32[1024,256]{1,0:T(8,128)} async-done(((f32[4096,256]{1,0:T(8,128)}), f32[1024,256]{1,0:T(8,128)}) %reduce-scatter.2.cloned.1.call-update) | async-done | bytes 1048592 | tf_op jit(solution)/shard_map/reduce_scatter | solution.py:96
  656.0 2.8 add_divide_fusion
  (88 shorter events, 25.7 us)
Async XLA Ops:
  7.2 31.3 %copy-start = (bf16[1024,256]{1,0:T(8,128)(2,1)S(1)}, bf16[1024,256]{1,0:T(8,128)(2,1)}, u32[]{:S(2)}) copy-start(bf16[1024,256]{1,0:T(8,128)(2,1)} %param.14) | copy-start | bytes 1572868
  7.2 122.0 %all-gather.2.cloned.1.call-start = ((), (), s32[]{:S(2)}) async-start(), calls=%async_computation.1 | async-start | bytes 2162688 | tf_op jit(solution)/shard_map/all_gather | solution.py:86
  38.5 20.1 %copy-start.2 = (bf16[4096,256]{1,0:T(8,128)(2,1)S(1)}, bf16[4096,256]{1,0:T(8,128)(2,1)}, u32[]{:S(2)}) copy-start(bf16[4096,256]{1,0:T(8,128)(2,1)} %param.15) | copy-start | bytes 6291460
  57.6 598.4 %reduce-scatter.2.cloned.1.call-start = ((), (), s32[]{:S(2)}) async-start(), calls=%async_computation.2 | async-start | bytes 5242880 | tf_op jit(solution)/shard_map/reduce_scatter | solution.py:96
  58.6 1.6 copy-start.3
  558.2 1.6 copy-start.4
  559.8 2.3 copy-start.5
  559.8 99.0 %copy-start.1 = (bf16[1024,256]{1,0:T(8,128)(2,1)S(1)}, bf16[1024,256]{1,0:T(8,128)(2,1)}, u32[]{:S(2)}) copy-start(bf16[1024,256]{1,0:T(8,128)(2,1)} %param.14) | copy-start | bytes 1572868
Sparse Core Ops, SparseCore 0:
  57.7 71.4 all-gather.1
  558.3 97.5 reduce-scatter.1
where the time goes:
time: 667 us; the launch traced here: 666 us
  blocking collectives  371 us (56%)
  matrix products  135 us (20%)
  waiting for transfers between devices  91.5 us (14%)
  other arithmetic  26.8 us (4%)
  local copies, waits for them, and re-layouts  25.9 us (4%)
  between operations  14.8 us (2%)
    pmax x1, blocking collectives, local(): peak = lax.pmax(local_peak, 'code')  153 us
    psum x1, blocking collectives, local(): total = lax.psum(local_total * jnp.exp(local_peak - peak), 'code')  150 us
    all_gather x1, waiting for transfers between devices, local(): piece = lax.all_gather(unit_tokens, 'code', axis=0, tiled=True)  68.3 us
    unnamed x1, blocking collectives  68.3 us
    dot_general x8, matrix products, accumulate(): lax.dot_general(resp, token_block, (((0,), (0,)), ((), ())), preferred_el...  52.8 us
    dot_general x8, matrix products, accumulate(): jnp.dot(token_block, code_rows.T, preferred_element_type=jnp.float32)  38.9 us
    reduce_scatter x1, waiting for transfers between devices, local(): lax.psum_scatter(sums, 'dp', scatter_dimension=0, tiled=True)  23.1 us
    dot_general x8, matrix products, block_stats(): jnp.dot(token_block, unit_codes.T, preferred_element_type=jnp.float32)  18.6 us
  transfers between devices with their start and end apart: 2, of which 2 were waited for; matrix products, arithmetic and copies ran while one was open for 1% of the time, Pallas kernels for 0%

commit v1 on v0

--- a/solution.py
+++ b/solution.py
@@ -88,7 +88,7 @@
     local_peak = peak
     local_total = total
     peak = lax.pmax(local_peak, "code")
-    total = lax.psum(local_total * jnp.exp(local_peak - peak), "code")
+    total = jnp.sum(lax.all_gather(local_total * jnp.exp(local_peak - peak), "code"), axis=0)
     lognorm = peak + jnp.log(total)
     owned = codebook.shape[0] // lax.axis_size("dp")
     sums, mass = weighted_sums(piece, group_scale, lognorm, unit_codes)

time: 667 us -> 584 us (0.88)
  blocking collectives: 371 us -> 286 us
    psum x1 -> x0, blocking collectives: 150 us -> none  [local(): total = lax.psum(local_total * jnp.exp(local_peak - peak), 'code')]
    all_gather x0 -> x1, blocking collectives: none -> 77.5 us  [local(): lax.all_gather(local_total * jnp.exp(local_peak - peak), 'code')]
    unnamed x1, blocking collectives: 68.3 us -> 55 us
where the time goes in v1:
time: 584 us; the launch traced here: 583 us
  blocking collectives  286 us (49%)
  matrix products  135 us (23%)
  waiting for transfers between devices  94.3 us (16%)
  other arithmetic  26.9 us (5%)
  local copies, waits for them, and re-layouts  26 us (4%)
  between operations  14.9 us (3%)
    pmax x1, blocking collectives, local(): peak = lax.pmax(local_peak, 'code')  153 us
    all_gather x1, blocking collectives, local(): lax.all_gather(local_total * jnp.exp(local_peak - peak), 'code')  77.5 us
    all_gather x1, waiting for transfers between devices, local(): piece = lax.all_gather(unit_tokens, 'code', axis=0, tiled=True)  68.3 us
    unnamed x1, blocking collectives  55 us
    dot_general x8, matrix products, accumulate(): lax.dot_general(resp, token_block, (((0,), (0,)), ((), ())), preferred_el...  52.8 us
    dot_general x8, matrix products, accumulate(): jnp.dot(token_block, code_rows.T, preferred_element_type=jnp.float32)  38.9 us
    reduce_scatter x1, waiting for transfers between devices, local(): lax.psum_scatter(sums, 'dp', scatter_dimension=0, tiled=True)  25.9 us
    dot_general x8, matrix products, block_stats(): jnp.dot(token_block, unit_codes.T, preferred_element_type=jnp.float32)  18.6 us
  transfers between devices with their start and end apart: 2, of which 2 were waited for; matrix products, arithmetic and copies ran while one was open for 1% of the time, Pallas kernels for 0%

profile of v1, /device:TPU:1, one launch (start us, length us, event | category | flops | bytes accessed | tf_op | source)
XLA Modules:
  0.0 583.3 jit_solution(15791395720831651153)
XLA Ops:
  10.5 6.2 %fusion.28 = f32[128,4096]{1,0:T(8,128)} fusion(bf16[1024,4096]{1,0:T(8,128)(2,1)} %param.12, bf16[128,1024]{1,0:T(8,128)(2,1)} %param.11, f32[128]{0:T(128)S(1)} %add_rsqrt_fusion.1, f32[128]{0:T(128)S(1)} %broadcast_multiply_fusion), kind=kOutput, calls=%fused_computation.50 | convolution fusion | flops 1074266112 | bytes 10748928 | tf_op jit(solution)/shard_map/dot_general | solution.py:15
  22.9 1.6 erfc.277
  26.0 1.6 erfc.283
  27.6 1.6 erfc.286
  30.8 1.6 erfc.292
  35.4 1.6 mul.100
  38.5 18.3 %multiply_reduce_fusion.2 = (f32[128]{0:T(128)S(1)}, f32[128,256]{1,0:T(8,128)S(1)}) fusion(bf16[1024,256]{1,0:T(8,128)(2,1)S(1)} %copy-done, f32[128,1024]{1,0:T(8,128)S(1)} %convert_element_type.28, bf16[4096,1024]{1,0:T(8,128)(2,1)} %param.13, f32[128,4096]{1,0:T(8,128)} %erfc.292, f32[128,4096]{1,0:T(8,128)} %erfc.290, f32[128,4096]{1,0:T(8,128)} %erfc.301, ...), kind=kOutput, calls=%fused_computation.54 | convolution fusion | flops 1175256960 | bytes 41026048 | tf_op jit(solution)/shard_map/dot_general | solution.py:20
  60.9 68.3 %all-gather.3.cloned.1.call-done = bf16[4096,256]{1,0:T(8,128)(2,1)} async-done(((bf16[128,256]{1,0:T(8,128)(2,1)}), bf16[4096,256]{1,0:T(8,128)(2,1)}) %all-gather.3.cloned.1.call-update) | async-done | bytes 2097168 | tf_op jit(solution)/shard_map/all_gather | solution.py:86
  129.2 34.2 %while.25 = (s32[]{:T(128)}, f32[8,512]{1,0:T(8,128)S(1)}, f32[8,512]{1,0:T(8,128)S(1)}, bf16[8,512,256]{2,1,0:T(8,128)(2,1)}, bf16[4096,256]{1,0:T(8,128)(2,1)S...) while((s32[]{:T(128)}, f32[8,512]{1,0:T(8,128)S(1)}, f32[8,512]{1,0:T(8,128)S(1)}, ...), condition=%wide.region_7.8_spmd, body=%wide.region_4.7_spmd.sunk | while | flops 1084226560 | bytes 19159648 | solution.py:30
  129.2 2.3 multiply_reduce_fusion.4
  131.6 1.8 exponential_reduce_fusion.2
  133.5 2.3 multiply_reduce_fusion.4
  135.8 1.8 exponential_reduce_fusion.2
  137.8 2.3 multiply_reduce_fusion.4
  140.1 1.8 exponential_reduce_fusion.2
  142.1 2.3 multiply_reduce_fusion.4
  144.4 1.8 exponential_reduce_fusion.2
  146.3 2.3 multiply_reduce_fusion.4
  148.7 1.8 exponential_reduce_fusion.2
  150.6 2.3 multiply_reduce_fusion.4
  153.0 1.8 exponential_reduce_fusion.2
  154.9 2.3 multiply_reduce_fusion.4
  157.2 1.8 exponential_reduce_fusion.2
  159.2 2.3 multiply_reduce_fusion.4
  161.5 1.8 exponential_reduce_fusion.2
  163.5 153.2 %pmax.7 = f32[4096]{0:T(1024)S(1)} all-reduce(f32[4096]{0:T(1024)S(1)} %bitcast.56), channel_id=1, replica_groups=mesh['dp'=4,'code'=32] {'code'}, use_global_device_ids=true, to_apply=%region_8.9 | all-reduce | flops 4096 | bytes 32768 | tf_op jit(solution)/shard_map/pmax | solution.py:90
  316.7 77.5 %all-gather = f32[131072]{0:T(1024)S(1)} all-gather(f32[4096]{0:T(1024)S(1)} %exponential_multiply_fusion), channel_id=2, replica_groups=mesh['dp'=4,'code'=32] {'code'}, dimensions={0}, use_global_device_ids=true | all-gather | bytes 540672 | tf_op jit(solution)/shard_map/all_gather | solution.py:91
  394.4 91.9 %while.26 = (s32[]{:T(128)}, f32[4096,256]{1,0:T(8,128)}, f32[4096]{0:T(1024)S(1)}, bf16[8,512,256]{2,1,0:T(8,128)(2,1)}, bf16[4096,256]{1,0:T(8,128)(2,1)S(1)},...) while((s32[]{:T(128)}, f32[4096,256]{1,0:T(8,128)}, ...), condition=%wide.region_12.13_spmd.clone, body=%wide.region_10.12_spmd.clone.sunk | while | flops 2160070656 | bytes 19477612 | solution.py:62
  394.4 4.9 convert_reduce_fusion.3
  399.3 5.4 convolution_add_fusion.3
  404.8 4.9 convert_reduce_fusion.3
  409.6 6.8 %convolution_add_fusion.3 = f32[4096,256]{1,0:T(8,128)} fusion(bf16[512,4096]{1,0:T(8,128)(2,1)} %get-tuple-element.228, f32[4096,256]{1,0:T(8,128)} %get-tuple-element.264, pred[]{:T(512)S(6)} %compare.3, bf16[8,512,256]{2,1,0:T(8,128)(2,1)} %get-tuple-element.275, s32[]{:T(128)} %get-tuple-element.263), kind=kOutput, calls=%fused_computation.9.clone.1 | convolution fusion | flops 1075838976 | bytes 12845569 | tf_op jit(solution)/shard_map/while/body/eval_jaxpr/dot_general | solution.py:47
  416.4 4.9 convert_reduce_fusion.3
  421.3 6.8 %convolution_add_fusion.3 = f32[4096,256]{1,0:T(8,128)} fusion(bf16[512,4096]{1,0:T(8,128)(2,1)} %get-tuple-element.228, f32[4096,256]{1,0:T(8,128)} %get-tuple-element.264, pred[]{:T(512)S(6)} %compare.3, bf16[8,512,256]{2,1,0:T(8,128)(2,1)} %get-tuple-element.275, s32[]{:T(128)} %get-tuple-element.263), kind=kOutput, calls=%fused_computation.9.clone.1 | convolution fusion | flops 1075838976 | bytes 12845569 | tf_op jit(solution)/shard_map/while/body/eval_jaxpr/dot_general | solution.py:47
  428.1 4.9 convert_reduce_fusion.3
  432.9 6.8 %convolution_add_fusion.3 = f32[4096,256]{1,0:T(8,128)} fusion(bf16[512,4096]{1,0:T(8,128)(2,1)} %get-tuple-element.228, f32[4096,256]{1,0:T(8,128)} %get-tuple-element.264, pred[]{:T(512)S(6)} %compare.3, bf16[8,512,256]{2,1,0:T(8,128)(2,1)} %get-tuple-element.275, s32[]{:T(128)} %get-tuple-element.263), kind=kOutput, calls=%fused_computation.9.clone.1 | convolution fusion | flops 1075838976 | bytes 12845569 | tf_op jit(solution)/shard_map/while/body/eval_jaxpr/dot_general | solution.py:47
  439.7 4.9 convert_reduce_fusion.3
  444.6 6.8 %convolution_add_fusion.3 = f32[4096,256]{1,0:T(8,128)} fusion(bf16[512,4096]{1,0:T(8,128)(2,1)} %get-tuple-element.228, f32[4096,256]{1,0:T(8,128)} %get-tuple-element.264, pred[]{:T(512)S(6)} %compare.3, bf16[8,512,256]{2,1,0:T(8,128)(2,1)} %get-tuple-element.275, s32[]{:T(128)} %get-tuple-element.263), kind=kOutput, calls=%fused_computation.9.clone.1 | convolution fusion | flops 1075838976 | bytes 12845569 | tf_op jit(solution)/shard_map/while/body/eval_jaxpr/dot_general | solution.py:47
  451.3 4.9 convert_reduce_fusion.3
  456.2 6.8 %convolution_add_fusion.3 = f32[4096,256]{1,0:T(8,128)} fusion(bf16[512,4096]{1,0:T(8,128)(2,1)} %get-tuple-element.228, f32[4096,256]{1,0:T(8,128)} %get-tuple-element.264, pred[]{:T(512)S(6)} %compare.3, bf16[8,512,256]{2,1,0:T(8,128)(2,1)} %get-tuple-element.275, s32[]{:T(128)} %get-tuple-element.263), kind=kOutput, calls=%fused_computation.9.clone.1 | convolution fusion | flops 1075838976 | bytes 12845569 | tf_op jit(solution)/shard_map/while/body/eval_jaxpr/dot_general | solution.py:47
  463.0 4.9 convert_reduce_fusion.3
  467.9 6.8 %convolution_add_fusion.3 = f32[4096,256]{1,0:T(8,128)} fusion(bf16[512,4096]{1,0:T(8,128)(2,1)} %get-tuple-element.228, f32[4096,256]{1,0:T(8,128)} %get-tuple-element.264, pred[]{:T(512)S(6)} %compare.3, bf16[8,512,256]{2,1,0:T(8,128)(2,1)} %get-tuple-element.275, s32[]{:T(128)} %get-tuple-element.263), kind=kOutput, calls=%fused_computation.9.clone.1 | convolution fusion | flops 1075838976 | bytes 12845569 | tf_op jit(solution)/shard_map/while/body/eval_jaxpr/dot_general | solution.py:47
  474.6 4.9 convert_reduce_fusion.3
  479.5 6.8 %convolution_add_fusion.3 = f32[4096,256]{1,0:T(8,128)} fusion(bf16[512,4096]{1,0:T(8,128)(2,1)} %get-tuple-element.228, f32[4096,256]{1,0:T(8,128)} %get-tuple-element.264, pred[]{:T(512)S(6)} %compare.3, bf16[8,512,256]{2,1,0:T(8,128)(2,1)} %get-tuple-element.275, s32[]{:T(128)} %get-tuple-element.263), kind=kOutput, calls=%fused_computation.9.clone.1 | convolution fusion | flops 1075838976 | bytes 12845569 | tf_op jit(solution)/shard_map/while/body/eval_jaxpr/dot_general | solution.py:47
  487.9 2.3 convert_element_type.27
  491.4 55.0 %all-reduce = f32[4096]{0:T(1024)S(1)} all-reduce(f32[4096]{0:T(1024)S(1)} %get-tuple-element.76), channel_id=4, replica_groups=mesh['dp'=4,'code'=32] {'dp'}, use_global_device_ids=true, to_apply=%region_14.15.clone | all-reduce | flops 4096 | bytes 32768
  547.7 25.9 %reduce-scatter.2.cloned.1.call-done = f32[1024,256]{1,0:T(8,128)} async-done(((f32[4096,256]{1,0:T(8,128)}), f32[1024,256]{1,0:T(8,128)}) %reduce-scatter.2.cloned.1.call-update) | async-done | bytes 1048592 | tf_op jit(solution)/shard_map/reduce_scatter | solution.py:96
  573.6 2.8 add_divide_fusion
  (90 shorter events, 25.9 us)
Async XLA Ops:
  7.2 31.3 %copy-start = (bf16[1024,256]{1,0:T(8,128)(2,1)S(1)}, bf16[1024,256]{1,0:T(8,128)(2,1)}, u32[]{:S(2)}) copy-start(bf16[1024,256]{1,0:T(8,128)(2,1)} %param.14) | copy-start | bytes 1572868
  7.2 122.0 %all-gather.3.cloned.1.call-start = ((), (), s32[]{:S(2)}) async-start(), calls=%async_computation.1 | async-start | bytes 2162688 | tf_op jit(solution)/shard_map/all_gather | solution.py:86
  38.5 20.1 %copy-start.2 = (bf16[4096,256]{1,0:T(8,128)(2,1)S(1)}, bf16[4096,256]{1,0:T(8,128)(2,1)}, u32[]{:S(2)}) copy-start(bf16[4096,256]{1,0:T(8,128)(2,1)} %param.15) | copy-start | bytes 6291460
  57.6 516.0 %reduce-scatter.2.cloned.1.call-start = ((), (), s32[]{:S(2)}) async-start(), calls=%async_computation.2 | async-start | bytes 5242880 | tf_op jit(solution)/shard_map/reduce_scatter | solution.py:96
  58.6 1.6 copy-start.3
  486.3 1.6 copy-start.4
  487.9 2.3 copy-start.5
  487.9 88.6 %copy-start.1 = (bf16[1024,256]{1,0:T(8,128)(2,1)S(1)}, bf16[1024,256]{1,0:T(8,128)(2,1)}, u32[]{:S(2)}) copy-start(bf16[1024,256]{1,0:T(8,128)(2,1)} %param.14) | copy-start | bytes 1572868
Sparse Core Ops, SparseCore 0:
  57.7 71.4 all-gather.2
  486.4 87.1 reduce-scatter.1
